TPU v7x, 32 devices: a whole 2x2x4 slice. The times are simulated.
32 devices in a mesh: fsdp: 8 (over z, x), ctx: 4 (over y, core).
Axes of the slice: x: 2, y: 2, z: 4, core: 2. Of those that a mesh axis runs over, the one named last changes fastest.
Arguments:
- tokens: bfloat16 [16, 592, 1024], P('fsdp', 'ctx'), may hold values from -6 to 6
- out_grad: bfloat16 [16, 592, 1024], P('fsdp', 'ctx'), may hold values from -6 to 6
- key_mask: int32 [16, 592], P('fsdp', 'ctx'), may hold values from 0 to 1, as said below
- slot_valid: int32 [16], P('fsdp'), may hold values 0 or 1
- norm_gains: bfloat16 [2, 1024], P(None, 'fsdp'), may hold values from 0.25 to 1.75
- norm_shifts: bfloat16 [2, 1024], P(None, 'fsdp'), may hold values from -2 to 2
- qkv_weight: bfloat16 [1024, 3072], P('fsdp'), may hold values from -0.1875 to 0.1875
- qv_bias: bfloat16 [2, 1024], P(None, 'fsdp'), may hold values from -3 to 3
- out_weight: bfloat16 [1024, 1024], P('fsdp'), may hold values from -1.5 to 1.5
- out_bias: bfloat16 [1024], P('fsdp'), may hold values from -2 to 2
- fc1_weight: bfloat16 [1024, 4096], P('fsdp'), may hold values from -0.1875 to 0.1875
- fc1_bias: bfloat16 [4096], P('fsdp'), may hold values from -3 to 3
- fc2_weight: bfloat16 [4096, 1024], P('fsdp'), may hold values from -0.125 to 0.125
- fc2_bias: bfloat16 [1024], P('fsdp'), may hold values from -2 to 2
Outputs:
- result: bfloat16 [16, 592, 1024], P('fsdp', 'ctx')
- token_gradient: bfloat16 [16, 592, 1024], P('fsdp', 'ctx')
- gain_grads: float32 [2, 1024], P(None, 'fsdp')
- shift_grads: float32 [2, 1024], P(None, 'fsdp')
- qkv_grad: float32 [1024, 3072], P('fsdp')
- qv_bias_grad: float32 [2, 1024], P(None, 'fsdp')
- out_weight_grad: float32 [1024, 1024], P('fsdp')
- out_bias_grad: float32 [1024], P('fsdp')
- fc1_grad: float32 [1024, 4096], P('fsdp')
- fc1_bias_grad: float32 [4096], P('fsdp')
- fc2_grad: float32 [4096, 1024], P('fsdp')
- fc2_bias_grad: float32 [1024], P('fsdp')
Inputs may be any that keep to these rules, and one draw needn't show every extreme that they name: key_mask is 1 at position 0 of every image and 0 at positions 577 and beyond.
All inputs are finite; a program needn't handle non-finite values. No bound on the sum of `slot_valid` on one device may be relied on, other than what follows from the above.
Results may differ from a plain program's by a relative error of at most 0.017.
Values may be sent and summed in bfloat16 or wider, within the bound.
No kernel may reach another device: no remote copies, remote signals or barrier semaphores. Data moves between devices by JAX's collectives and lax.ppermute only.
A program may use at most 192 MiB of HBM per device.

v0:
```python
import jax
import jax.numpy as jnp
from jax import lax
from jax.sharding import PartitionSpec as P

D = 1024
HEADS = 16
HEAD_DIM = 64
LIVE = 577


def across_rows(left_side, right_side):
    return lax.dot_general(
        left_side, right_side, (((0,), (0,)), ((), ())), preferred_element_type=jnp.float32
    )


def against(left_side, right_side):
    return lax.dot_general(
        left_side, right_side, (((1,), (1,)), ((), ())), preferred_element_type=jnp.float32
    )


def apply_layer_norm(values, gain_row, shift_row):
    centred = values - jnp.mean(values, axis=-1, keepdims=True)
    inverse_std = lax.rsqrt(jnp.mean(centred * centred, axis=-1, keepdims=True) + 1e-05)
    normed = centred * inverse_std
    return (normed * gain_row + shift_row, normed, inverse_std)


def norm_reverse_pass(grad_normed, normed, inverse_std):
    first_mean = jnp.mean(grad_normed, axis=-1, keepdims=True)
    second_mean = jnp.mean(grad_normed * normed, axis=-1, keepdims=True)
    return inverse_std * (grad_normed - first_mean - normed * second_mean)


def head_slice(source, head_index, offset):
    return lax.dynamic_slice_in_dim(source, offset + head_index * HEAD_DIM, HEAD_DIM, 2)


def body(
    tokens,
    out_grad,
    key_mask,
    slot_valid,
    norm_gains,
    norm_shifts,
    qkv_weight,
    qv_bias,
    out_weight,
    out_bias,
    fc1_weight,
    fc1_bias,
    fc2_weight,
    fc2_bias,
):
    full_params = (
        lax.all_gather(norm_gains, "fsdp", axis=1, tiled=True),
        lax.all_gather(norm_shifts, "fsdp", axis=1, tiled=True),
        lax.all_gather(qkv_weight, "fsdp", axis=0, tiled=True),
        lax.all_gather(qv_bias, "fsdp", axis=1, tiled=True),
        lax.all_gather(out_weight, "fsdp", axis=0, tiled=True),
        lax.all_gather(out_bias, "fsdp", axis=0, tiled=True),
        lax.all_gather(fc1_weight, "fsdp", axis=0, tiled=True),
        lax.all_gather(fc1_bias, "fsdp", axis=0, tiled=True),
        lax.all_gather(fc2_weight, "fsdp", axis=0, tiled=True),
        lax.all_gather(fc2_bias, "fsdp", axis=0, tiled=True),
    )
    norm_gain_vector = full_params[0].astype(jnp.float32)
    norm_bias_vector = full_params[1].astype(jnp.float32)
    qkv_matrix = full_params[2]
    qv_shift = full_params[3].astype(jnp.float32)
    out_matrix = full_params[4]
    out_shift = full_params[5].astype(jnp.float32)
    fc1_matrix = full_params[6]
    fc1_shift = full_params[7].astype(jnp.float32)
    fc2_matrix = full_params[8]
    fc2_shift = full_params[9].astype(jnp.float32)
    image_count = tokens.shape[0]
    local_len = tokens.shape[1]
    row_count = image_count * local_len
    flattened_rows = tokens.reshape(row_count, D).astype(jnp.float32)
    normalized_input, first_centred_scaled, first_inverse_deviation = apply_layer_norm(
        flattened_rows, norm_gain_vector[0], norm_bias_vector[0]
    )
    normed_low = normalized_input.astype(jnp.bfloat16)
    raw_proj = jnp.dot(normed_low, qkv_matrix, preferred_element_type=jnp.float32)
    queries = (
        (raw_proj[:, :D] + qv_shift[0]).astype(jnp.bfloat16).reshape(image_count, local_len, D)
    )
    key_value = jnp.concatenate(
        [raw_proj[:, D : 2 * D], raw_proj[:, 2 * D :] + qv_shift[1]], axis=1
    )
    key_value = key_value.astype(jnp.bfloat16).reshape(image_count, local_len, 2 * D)
    key_all, mask_all = (
        lax.all_gather(key_value, "ctx", axis=1, tiled=True),
        lax.all_gather(key_mask.astype(jnp.bfloat16), "ctx", axis=1, tiled=True),
    )
    visible = (mask_all > 0)[:, None, :]

    def head_forward(head_index):
        head_queries = head_slice(queries, head_index, 0)
        head_keys = head_slice(key_all, head_index, 0)
        head_value_rows = head_slice(key_all, head_index, D)
        scores = (
            jnp.einsum("jgz,jaz->jga", head_queries, head_keys, preferred_element_type=jnp.float32)
            * 0.125
        )
        scores = jnp.where(visible, scores, -1e30)
        row_max = jnp.max(scores, axis=-1, keepdims=True)
        exponent = jnp.exp(scores - row_max)
        row_sum = jnp.sum(exponent, axis=-1, keepdims=True)
        attention_weights = (exponent / row_sum).astype(jnp.bfloat16)
        context = jnp.einsum(
            "ans,ash->anh", attention_weights, head_value_rows, preferred_element_type=jnp.float32
        )
        return (context.astype(jnp.bfloat16), (row_max + jnp.log(row_sum))[:, :, 0])

    contexts, log_norm = lax.map(head_forward, jnp.arange(HEADS))
    context_low = contexts.transpose(1, 2, 0, 3).reshape(row_count, D)
    residual_state = (
        flattened_rows
        + jnp.dot(context_low, out_matrix, preferred_element_type=jnp.float32)
        + out_shift
    )
    normalized_residual, second_centred_scaled, second_inverse_deviation = apply_layer_norm(
        residual_state, norm_gain_vector[1], norm_bias_vector[1]
    )
    middle_low = normalized_residual.astype(jnp.bfloat16)
    pre_act = jnp.dot(middle_low, fc1_matrix, preferred_element_type=jnp.float32) + fc1_shift
    sigmoid_gate = jax.nn.sigmoid(1.702 * pre_act)
    hidden = (pre_act * sigmoid_gate).astype(jnp.bfloat16)
    output = (
        residual_state + jnp.dot(hidden, fc2_matrix, preferred_element_type=jnp.float32) + fc2_shift
    )
    result = output.astype(jnp.bfloat16).reshape(image_count, local_len, D)
    position = lax.axis_index("ctx") * local_len + jnp.arange(local_len)
    keep_row = (position < LIVE)[None, :] & (slot_valid[:, None] > 0)
    grad_out = jnp.where(keep_row[:, :, None], out_grad, jnp.zeros_like(out_grad)).reshape(
        row_count, D
    )
    held = lax.optimization_barrier(
        ((norm_gains, qkv_weight, out_weight, fc1_weight, fc2_weight), grad_out)
    )
    held_gain, held_qkv, held_out, held_fc1, held_fc2 = held[0]
    again_params = (
        lax.all_gather(held_gain, "fsdp", axis=1, tiled=True),
        lax.all_gather(held_qkv, "fsdp", axis=0, tiled=True),
        lax.all_gather(held_out, "fsdp", axis=0, tiled=True),
        lax.all_gather(held_fc1, "fsdp", axis=0, tiled=True),
        lax.all_gather(held_fc2, "fsdp", axis=0, tiled=True),
    )
    reverse_gain_pass = again_params[0].astype(jnp.float32)
    back_qkv = again_params[1]
    back_out = again_params[2]
    back_fc1 = again_params[3]
    back_fc2 = again_params[4]
    grad_fc2 = across_rows(hidden, grad_out)
    grad_fc2_shift = jnp.sum(grad_out.astype(jnp.float32), axis=0)
    grad_hidden = against(grad_out, back_fc2)
    grad_pre = grad_hidden * (sigmoid_gate + 1.702 * pre_act * sigmoid_gate * (1.0 - sigmoid_gate))
    grad_fc1_shift = jnp.sum(grad_pre, axis=0)
    grad_pre_low = grad_pre.astype(jnp.bfloat16)
    grad_fc1 = across_rows(middle_low, grad_pre_low)
    middle_norm_gradient = against(grad_pre_low, back_fc1)
    second_gain_gradient = jnp.sum(middle_norm_gradient * second_centred_scaled, axis=0)
    grad_shift_two = jnp.sum(middle_norm_gradient, axis=0)
    residual_gradient = grad_out.astype(jnp.float32) + norm_reverse_pass(
        middle_norm_gradient * reverse_gain_pass[1], second_centred_scaled, second_inverse_deviation
    )
    grad_out_shift = jnp.sum(residual_gradient, axis=0)
    grad_middle_low = residual_gradient.astype(jnp.bfloat16)
    grad_out_matrix = across_rows(context_low, grad_middle_low)
    grad_context = (
        against(grad_middle_low, back_out).astype(jnp.bfloat16).reshape(image_count, local_len, D)
    )

    def head_backward(head_inputs):
        head_index, head_norm = head_inputs
        head_queries = head_slice(queries, head_index, 0)
        head_keys = head_slice(key_all, head_index, 0)
        head_value_rows = head_slice(key_all, head_index, D)
        head_gradient = head_slice(grad_context, head_index, 0)
        scores = (
            jnp.einsum("jgz,jaz->jga", head_queries, head_keys, preferred_element_type=jnp.float32)
            * 0.125
        )
        attention_weights = jnp.where(visible, jnp.exp(scores - head_norm[:, :, None]), 0.0)
        grad_probs = jnp.einsum(
            "jgz,jaz->jga", head_gradient, head_value_rows, preferred_element_type=jnp.float32
        )
        row_delta = jnp.sum(attention_weights * grad_probs, axis=-1, keepdims=True)
        score_gradient = (attention_weights * (grad_probs - row_delta)).astype(jnp.bfloat16)
        grad_query = (
            jnp.einsum(
                "ans,ash->anh", score_gradient, head_keys, preferred_element_type=jnp.float32
            )
            * 0.125
        )
        grad_key = (
            jnp.einsum(
                "isl,isc->ilc", score_gradient, head_queries, preferred_element_type=jnp.float32
            )
            * 0.125
        )
        grad_value = jnp.einsum(
            "isl,isc->ilc",
            attention_weights.astype(jnp.bfloat16),
            head_gradient,
            preferred_element_type=jnp.float32,
        )
        return (grad_query, grad_key, grad_value)

    grad_queries, grad_keys, grad_values = lax.map(head_backward, (jnp.arange(HEADS), log_norm))
    grad_keys_all = grad_keys.transpose(1, 2, 0, 3).reshape(image_count, -1, D)
    grad_values_all = grad_values.transpose(1, 2, 0, 3).reshape(image_count, -1, D)
    own_keys, own_values = (
        lax.psum_scatter(
            grad_keys_all.astype(jnp.bfloat16), "ctx", scatter_dimension=1, tiled=True
        ).astype(jnp.float32),
        lax.psum_scatter(
            grad_values_all.astype(jnp.bfloat16), "ctx", scatter_dimension=1, tiled=True
        ).astype(jnp.float32),
    )
    grad_query_rows = grad_queries.transpose(1, 2, 0, 3).reshape(row_count, D)
    own_value_rows = own_values.reshape(row_count, D)
    grad_qv_shift = jnp.stack([jnp.sum(grad_query_rows, axis=0), jnp.sum(own_value_rows, axis=0)])
    grad_raw = jnp.concatenate(
        [grad_query_rows, own_keys.reshape(row_count, D), own_value_rows], axis=1
    ).astype(jnp.bfloat16)
    grad_qkv = across_rows(normed_low, grad_raw)
    input_norm_gradient = against(grad_raw, back_qkv)
    first_gain_gradient = jnp.sum(input_norm_gradient * first_centred_scaled, axis=0)
    grad_shift_one = jnp.sum(input_norm_gradient, axis=0)
    token_gradient = residual_gradient + norm_reverse_pass(
        input_norm_gradient * reverse_gain_pass[0], first_centred_scaled, first_inverse_deviation
    )
    token_gradient = token_gradient.astype(jnp.bfloat16).reshape(image_count, local_len, D)
    grad_gains = jnp.stack([first_gain_gradient, second_gain_gradient])
    grad_shifts = jnp.stack([grad_shift_one, grad_shift_two])
    (
        gain_part,
        shift_part,
        qkv_part,
        qv_part,
        out_part,
        out_shift_part,
        fc1_part,
        fc1_shift_part,
        fc2_part,
        fc2_shift_part,
    ) = (
        lax.psum_scatter(grad_gains, "fsdp", scatter_dimension=1, tiled=True),
        lax.psum_scatter(grad_shifts, "fsdp", scatter_dimension=1, tiled=True),
        lax.psum_scatter(grad_qkv, "fsdp", scatter_dimension=0, tiled=True),
        lax.psum_scatter(grad_qv_shift, "fsdp", scatter_dimension=1, tiled=True),
        lax.psum_scatter(grad_out_matrix, "fsdp", scatter_dimension=0, tiled=True),
        lax.psum_scatter(grad_out_shift, "fsdp", scatter_dimension=0, tiled=True),
        lax.psum_scatter(grad_fc1, "fsdp", scatter_dimension=0, tiled=True),
        lax.psum_scatter(grad_fc1_shift, "fsdp", scatter_dimension=0, tiled=True),
        lax.psum_scatter(grad_fc2, "fsdp", scatter_dimension=0, tiled=True),
        lax.psum_scatter(grad_fc2_shift, "fsdp", scatter_dimension=0, tiled=True),
    )
    finished = (
        lax.psum(gain_part.astype(jnp.bfloat16), "ctx").astype(jnp.float32),
        lax.psum(shift_part.astype(jnp.bfloat16), "ctx").astype(jnp.float32),
        lax.psum(qkv_part.astype(jnp.bfloat16), "ctx").astype(jnp.float32),
        lax.psum(qv_part.astype(jnp.bfloat16), "ctx").astype(jnp.float32),
        lax.psum(out_part.astype(jnp.bfloat16), "ctx").astype(jnp.float32),
        lax.psum(out_shift_part.astype(jnp.bfloat16), "ctx").astype(jnp.float32),
        lax.psum(fc1_part.astype(jnp.bfloat16), "ctx").astype(jnp.float32),
        lax.psum(fc1_shift_part.astype(jnp.bfloat16), "ctx").astype(jnp.float32),
        lax.psum(fc2_part.astype(jnp.bfloat16), "ctx").astype(jnp.float32),
        lax.psum(fc2_shift_part.astype(jnp.bfloat16), "ctx").astype(jnp.float32),
    )
    return (
        result,
        token_gradient,
        finished[0],
        finished[1],
        finished[2],
        finished[3],
        finished[4],
        finished[5],
        finished[6],
        finished[7],
        finished[8],
        finished[9],
    )


def solution(mesh):
    in_specs = (
        P("fsdp", "ctx", None),
        P("fsdp", "ctx", None),
        P("fsdp", "ctx"),
        P("fsdp"),
        P(None, "fsdp"),
        P(None, "fsdp"),
        P("fsdp", None),
        P(None, "fsdp"),
        P("fsdp", None),
        P("fsdp"),
        P("fsdp", None),
        P("fsdp"),
        P("fsdp", None),
        P("fsdp"),
    )
    out_specs = (
        P("fsdp", "ctx", None),
        P("fsdp", "ctx", None),
        P(None, "fsdp"),
        P(None, "fsdp"),
        P("fsdp", None),
        P(None, "fsdp"),
        P("fsdp", None),
        P("fsdp"),
        P("fsdp", None),
        P("fsdp"),
        P("fsdp", None),
        P("fsdp"),
    )
    return jax.shard_map(body, mesh=mesh, in_specs=in_specs, out_specs=out_specs, check_vma=False)
```

profile of v0, /device:TPU:0, one launch (start us, length us, event | category | flops | bytes accessed | tf_op | source)
XLA Modules:
  0.0 2301.7 jit_solution(17001615898816371938)
XLA Ops:
  8.0 2.3 copy.94
  13.6 22.3 all_gather.53
  36.0 16.5 all_gather.52
  52.4 18.4 all_gather.55
  70.8 41.2 %all-gather.14.cloned.1.call-done = bf16[1024,3072]{1,0:T(8,128)(2,1)} async-done(((bf16[128,3072]{1,0:T(8,128)(2,1)}), bf16[1024,3072]{1,0:T(8,128)(2,1)}) %all-gather.14.cloned.1.call-update) | async-done | bytes 6291472 | tf_op jit(solution)/shard_map/all_gather | solution.py:60
  112.0 5.0 fusion.46
  120.5 2.3 copy.99
  127.8 17.6 all-gather.1
  145.4 5.1 all-gather
  150.7 26.1 %all-gather.2 = bf16[8,1,512]{2,1,0:T(2,128)(2,1)S(1)} all-gather(bf16[1,1,512]{2,1,0:T(2,128)(2,1)S(1)} %reshape.215), channel_id=1, replica_groups=mesh['fsdp'=8,'ctx'=4] {'fsdp'}, dimensions={0}, use_global_device_ids=true | all-gather | bytes 9216 | tf_op jit(solution)/shard_map/all_gather | solution.py:65
  176.8 16.7 all_gather.65
  194.2 11.7 copy.101
  205.9 88.4 %while.30 = (s32[]{:T(128)}, bf16[16,2,148,64]{2,3,1,0:T(8,128)(2,1)}, f32[16,2,148]{2,1,0:T(2,128)}, pred[2,1,592]{2,0,1:T(4,128)(4,1)S(1)}, s32[16]{0:T(128)S(...) while((s32[]{:T(128)}, ...), condition=%wide.region_5.6_spmd, body=%wide.region_2.5_spmd.sunk | while | flops 46279904 | bytes 2574702 | solution.py:119
  219.9 2.0 fusion.93
  231.0 2.0 fusion.93
  236.5 2.0 fusion.93
  242.0 2.0 fusion.93
  247.5 2.0 fusion.93
  253.0 2.0 fusion.93
  264.1 2.0 fusion.93
  269.7 2.0 fusion.93
  280.7 2.0 fusion.93
  294.3 2.2 copy.102
  298.2 2.7 fusion.54
  301.2 35.1 %all-gather.20.cloned.1.call-done = bf16[1024,4096]{1,0:T(8,128)(2,1)} async-done(((bf16[128,4096]{1,0:T(8,128)(2,1)}), bf16[1024,4096]{1,0:T(8,128)(2,1)}) %all-gather.20.cloned.1.call-update) | async-done | bytes 8388624 | tf_op jit(solution)/shard_map/all_gather | solution.py:64
  336.3 8.5 convolution_add_fusion
  344.8 116.7 %all-gather.24.cloned.1.call-done = bf16[4096,1024]{1,0:T(8,128)(2,1)} async-done(((bf16[512,1024]{1,0:T(8,128)(2,1)}), bf16[4096,1024]{1,0:T(8,128)(2,1)}) %all-gather.24.cloned.1.call-update) | async-done | bytes 8388624 | tf_op jit(solution)/shard_map/all_gather | solution.py:151
  461.4 10.3 fusion.55
  471.7 114.9 %all-gather.26.cloned.1.call-done = bf16[1024,4096]{1,0:T(8,128)(2,1)} async-done(((bf16[128,4096]{1,0:T(8,128)(2,1)}), bf16[1024,4096]{1,0:T(8,128)(2,1)}) %all-gather.26.cloned.1.call-update) | async-done | bytes 8388624 | tf_op jit(solution)/shard_map/all_gather | solution.py:150
  586.6 6.5 multiply_reduce_fusion.1
  594.7 41.5 %all-gather.28.cloned.1.call-done = bf16[1024,1024]{1,0:T(8,128)(2,1)} async-done(((bf16[128,1024]{1,0:T(8,128)(2,1)}), bf16[1024,1024]{1,0:T(8,128)(2,1)}) %all-gather.28.cloned.1.call-update) | async-done | bytes 2097168 | tf_op jit(solution)/shard_map/all_gather | solution.py:149
  636.2 3.6 convolution_convert_fusion.1
  639.8 2.0 reshape.205
  641.8 2.2 copy.106
  644.0 165.1 %while.31 = (s32[]{:T(128)}, f32[16,2,148,64]{2,3,1,0:T(8,128)}, bf16[16,2,592,64]{2,3,1,0:T(8,128)(2,1)}, bf16[16,2,592,64]{2,3,1,0:T(8,128)(2,1)}, pred[2,1,59...) while((s32[]{:T(128)}, f32[16,2,148,64]{2,3,1,0:T(8,128)}, ...), condition=%wide.region_12.13_spmd, body=%wide.region_10.12_spmd.sunk | while | flops 113820000 | bytes 11654198 | solution.py:214
  809.2 3.5 copy.108
  812.7 6.6 copy.109
  819.3 3.5 copy.111
  822.8 6.6 copy.112
  830.4 4.6 fusion.42
  840.6 2.1 reshape.206
  843.6 80.8 %all-reduce.14.cloned.1.call-done = (bf16[2,592,1024]{2,0,1:T(2,128)(2,1)}, bf16[2,592,1024]{2,0,1:T(2,128)(2,1)}) async-done(((bf16[2,592,1024]{2,0,1:T(2,128)(2,1)}, bf16[2,592,1024]{2,0,1:T(2,128)(2,1)}), (bf16[2,592,1024]{2,0,1:T(2,128)(2,1)}, bf16[2,592,1024]{2,0,1:T(2,128)(2,1)})) %all-reduce.14.cloned.1.call-update) | async-done | bytes 4849680
  933.9 8.3 fusion.45
  942.2 10.3 fusion.38
  953.6 10.7 fusion.47
  966.9 58.9 %all-gather.30.cloned.1.call-done = bf16[1024,3072]{1,0:T(8,128)(2,1)} async-done(((bf16[128,3072]{1,0:T(8,128)(2,1)}), bf16[1024,3072]{1,0:T(8,128)(2,1)}) %all-gather.30.cloned.1.call-update) | async-done | bytes 6291472 | tf_op jit(solution)/shard_map/all_gather | solution.py:148
  1025.8 6.7 multiply_reduce_fusion.2
  1035.8 18.2 all-gather.3
  1056.0 59.5 %reduce-scatter.16.cloned.1.call-done = f32[128,1024]{1,0:T(8,128)} async-done(((f32[1024,1024]{1,0:T(8,128)}), f32[128,1024]{1,0:T(8,128)}) %reduce-scatter.16.cloned.1.call-update) | async-done | bytes 524304 | tf_op jit(solution)/shard_map/reduce_scatter | solution.py:257
  1117.2 209.3 %reduce-scatter.14.cloned.1.call-done = f32[128,3072]{1,0:T(8,128)} async-done(((f32[1024,3072]{1,0:T(8,128)}), f32[128,3072]{1,0:T(8,128)}) %reduce-scatter.14.cloned.1.call-update) | async-done | bytes 1572880 | tf_op jit(solution)/shard_map/reduce_scatter | solution.py:255
  1326.5 2.4 convert_element_type.208
  1328.9 283.5 %reduce-scatter.18.cloned.1.call-done = f32[128,4096]{1,0:T(8,128)} async-done(((f32[1024,4096]{1,0:T(8,128)}), f32[128,4096]{1,0:T(8,128)}) %reduce-scatter.18.cloned.1.call-update) | async-done | bytes 2097168 | tf_op jit(solution)/shard_map/reduce_scatter | solution.py:259
  1612.4 2.7 convert_element_type.217
  1615.1 282.9 %reduce-scatter.20.cloned.1.call-done = f32[512,1024]{1,0:T(8,128)} async-done(((f32[4096,1024]{1,0:T(8,128)}), f32[512,1024]{1,0:T(8,128)}) %reduce-scatter.20.cloned.1.call-update) | async-done | bytes 2097168 | tf_op jit(solution)/shard_map/reduce_scatter | solution.py:261
  1898.0 2.8 convert_element_type.221
  1900.8 123.4 %all-gather.22.cloned.1.call-done = bf16[4096,1024]{1,0:T(8,128)(2,1)} async-done(((bf16[512,1024]{1,0:T(8,128)(2,1)}), bf16[4096,1024]{1,0:T(8,128)(2,1)}) %all-gather.22.cloned.1.call-update) | async-done | bytes 8388624 | tf_op jit(solution)/shard_map/all_gather | solution.py:66
  2024.2 8.5 fusion.35
  2035.5 34.2 %all-reduce.5 = (bf16[1024]{0:T(1024)(128)(2,1)S(1)}, bf16[4096]{0:T(1024)(128)(2,1)S(1)}, bf16[1024]{0:T(1024)(128)(2,1)S(1)}) all-reduce(f32[1024]{0:T(1024)S(1)} %get-tuple-element.448, f32[4096]{0:T(1024)S(1)} %get-tuple-element.470, f32[1024]{0:T(1024)S(1)} %get-tuple-element.446), channel_id=9, replica_groups=mesh['fsdp'=8,'ctx'=4] {'fsdp'}, use_global_device_ids=true, to_apply=%region_34.35.clone | all-reduce | flops 6144 | bytes 36864
  2073.2 15.2 reduce-scatter.22.cloned.1.call-done
  2089.3 63.3 %reduce-scatter.24.cloned.1.call-done = f32[128,2]{1,0:T(8,128)} async-done(((f32[1024,2]{1,0:T(8,128)}), f32[128,2]{1,0:T(8,128)}) %reduce-scatter.24.cloned.1.call-update) | async-done | bytes 1040
  2153.5 63.5 %reduce-scatter.26.cloned.1.call-done = f32[128,2]{1,0:T(8,128)} async-done(((f32[1024,2]{1,0:T(8,128)}), f32[128,2]{1,0:T(8,128)}) %reduce-scatter.26.cloned.1.call-update) | async-done | bytes 1040
  2218.0 5.7 all-reduce.6
  2226.9 61.3 %all-reduce.12.cloned.1.call-done = (bf16[128,3072]{1,0:T(8,128)(2,1)}, bf16[128,1024]{1,0:T(8,128)(2,1)}, bf16[128,4096]{1,0:T(8,128)(2,1)}, bf16[512,1024]{1,0:T(8,128)(2,1)}) async-done(((bf16[128,3072]{1,0:T(8,128)(2,1)}, bf16[128,1024]{1,0:T(8,128)(2,1)}, bf16[128,4096]{1,0:T(8,128)(2,1)}, bf16[512,1024]{1,0:T(8,128)(2,1)}), (bf16[128,3072]{1,0:T(8,128)(2,1)}, bf16[128,1024]{1,0:T(8,128)(2,1)}, ...) | async-done | bytes 3145744 | tf_op jit(solution)/shard_map/psum | solution.py:267
  2288.2 2.5 convert_element_type.209
  (432 shorter events, 272.1 us)
Async XLA Ops:
  7.2 104.9 %all-gather.14.cloned.1.call-start = ((), (), s32[]{:S(2)}) async-start(), calls=%async_computation.7 | async-start | bytes 7077888 | tf_op jit(solution)/shard_map/all_gather | solution.py:60
  7.9 3.9 copy-start.1
  7.9 186.2 %all-gather.16.cloned.1.call-start = ((), (), s32[]{:S(2)}) async-start(), calls=%async_computation.8 | async-start | bytes 6062080 | tf_op jit(solution)/shard_map/all_gather | solution.py:96
  10.3 3.3 copy-start.15
  10.3 25.7 %copy-start.12 = (bf16[2,128]{1,0:T(2,128)(2,1)S(1)}, bf16[2,128]{1,0:T(2,128)(2,1)}, u32[]{:S(2)}) copy-start(bf16[2,128]{1,0:T(2,128)(2,1)} %param.22) | copy-start | bytes 1540
  10.3 42.1 %copy-start.16 = (bf16[2,128]{1,0:T(2,128)(2,1)S(1)}, bf16[2,128]{1,0:T(2,128)(2,1)}, u32[]{:S(2)}) copy-start(bf16[2,128]{1,0:T(2,128)(2,1)} %param.25) | copy-start | bytes 1540
  122.8 1.4 copy-start.19
  122.8 1.5 copy-start.10
  122.8 175.4 %all-gather.18.cloned.1.call-start = ((), (), s32[]{:S(2)}) async-start(), calls=%async_computation.9 | async-start | bytes 2359296 | tf_op jit(solution)/shard_map/all_gather | solution.py:62
  123.5 212.7 %all-gather.20.cloned.1.call-start = ((), (), s32[]{:S(2)}) async-start(), calls=%async_computation.10 | async-start | bytes 9437184 | tf_op jit(solution)/shard_map/all_gather | solution.py:64
  124.1 337.3 %all-gather.24.cloned.1.call-start = ((), (), s32[]{:S(2)}) async-start(), calls=%async_computation.12 | async-start | bytes 9437184 | tf_op jit(solution)/shard_map/all_gather | solution.py:151
  125.4 2.4 copy-start.17
  125.4 20.1 copy-start.13
  125.4 25.3 %copy-start.14 = (bf16[512]{0:T(512)(128)(2,1)S(1)}, bf16[512]{0:T(512)(128)(2,1)}, u32[]{:S(2)}) copy-start(bf16[512]{0:T(512)(128)(2,1)} %param.29) | copy-start | bytes 3076
  125.4 68.1 %copy-start.5 = (bf16[296,1024]{1,0:T(8,128)(2,1)S(1)}, bf16[296,1024]{1,0:T(8,128)(2,1)}, u32[]{:S(2)}) copy-start(bf16[296,1024]{1,0:T(8,128)(2,1)} %get-tuple-element.457) | copy-start | bytes 1818628
  126.4 460.2 %all-gather.26.cloned.1.call-start = ((), (), s32[]{:S(2)}) async-start(), calls=%async_computation.13 | async-start | bytes 9437184 | tf_op jit(solution)/shard_map/all_gather | solution.py:150
  127.0 509.2 %all-gather.28.cloned.1.call-start = ((), (), s32[]{:S(2)}) async-start(), calls=%async_computation.14 | async-start | bytes 2359296 | tf_op jit(solution)/shard_map/all_gather | solution.py:149
  127.7 796.7 %all-reduce.14.cloned.1.call-start = ((), (), s32[]{:S(2)}) async-start(), calls=%async_computation.24 | async-start | bytes 9699328
  586.6 6.6 copy-start.6
  649.0 5.4 copy-start.3
  654.4 1.3 copy-start.2
  659.3 5.4 copy-start.3
  664.7 1.3 copy-start.2
  669.6 5.4 copy-start.3
  675.0 1.3 copy-start.2
  679.9 5.4 copy-start.3
  685.3 1.3 copy-start.2
  690.2 5.4 copy-start.3
  695.7 1.3 copy-start.2
  700.6 5.4 copy-start.3
  706.0 1.3 copy-start.2
  710.9 5.4 copy-start.3
  716.3 1.3 copy-start.2
  721.2 5.4 copy-start.3
  731.5 5.4 copy-start.3
  741.8 5.4 copy-start.3
  747.2 1.3 copy-start.2
  752.1 5.4 copy-start.3
  757.5 1.3 copy-start.2
  762.4 5.4 copy-start.3
  767.8 1.3 copy-start.2
  772.8 5.4 copy-start.3
  778.2 1.3 copy-start.2
  783.1 5.4 copy-start.3
  788.5 1.3 copy-start.2
  793.4 5.4 copy-start.3
  798.8 1.3 copy-start.2
  803.8 5.4 copy-start.3
  829.4 196.4 %all-gather.30.cloned.1.call-start = ((), (), s32[]{:S(2)}) async-start(), calls=%async_computation.15 | async-start | bytes 7077888 | tf_op jit(solution)/shard_map/all_gather | solution.py:148
  830.1 285.3 %reduce-scatter.16.cloned.1.call-start = ((), (), s32[]{:S(2)}) async-start(), calls=%async_computation.17 | async-start | bytes 4718592 | tf_op jit(solution)/shard_map/reduce_scatter | solution.py:257
  835.0 491.5 %reduce-scatter.14.cloned.1.call-start = ((), (), s32[]{:S(2)}) async-start(), calls=%async_computation.16 | async-start | bytes 14155776 | tf_op jit(solution)/shard_map/reduce_scatter | solution.py:255
  942.2 670.2 %reduce-scatter.18.cloned.1.call-start = ((), (), s32[]{:S(2)}) async-start(), calls=%async_computation.18 | async-start | bytes 18874368 | tf_op jit(solution)/shard_map/reduce_scatter | solution.py:259
  952.6 945.4 %reduce-scatter.20.cloned.1.call-start = ((), (), s32[]{:S(2)}) async-start(), calls=%async_computation.19 | async-start | bytes 18874368 | tf_op jit(solution)/shard_map/reduce_scatter | solution.py:261
  964.4 1059.8 %all-gather.22.cloned.1.call-start = ((), (), s32[]{:S(2)}) async-start(), calls=%async_computation.11 | async-start | bytes 9437184 | tf_op jit(solution)/shard_map/all_gather | solution.py:66
  965.0 1123.5 %reduce-scatter.22.cloned.1.call-start = ((), (), s32[]{:S(2)}) async-start(), calls=%async_computation.20 | async-start | bytes 589824
  1032.5 3.4 copy-start.18
  1032.5 21.6 copy-start.20
  1033.5 1119.1 %reduce-scatter.24.cloned.1.call-start = ((), (), s32[]{:S(2)}) async-start(), calls=%async_computation.21 | async-start | bytes 589824
  1034.7 1182.4 %reduce-scatter.26.cloned.1.call-start = ((), (), s32[]{:S(2)}) async-start(), calls=%async_computation.22 | async-start | bytes 589824
  1035.8 1252.4 %all-reduce.12.cloned.1.call-start = ((), (), s32[]{:S(2)}) async-start(), calls=%async_computation.23 | async-start | bytes 6291456 | tf_op jit(solution)/shard_map/psum | solution.py:267
  2032.7 37.2 %copy-start = (f32[296,1024]{1,0:T(8,128)S(1)}, f32[296,1024]{1,0:T(8,128)}, u32[]{:S(2)}) copy-start(f32[296,1024]{1,0:T(8,128)} %get-tuple-element.449) | copy-start | bytes 3637252
  2288.2 2.5 copy-start.11
  2288.2 3.4 copy-start.9
  2290.7 2.4 copy-start.8
  (6 other events, 6.8 us)
Sparse Core Ops, SparseCore 0:
  10.2 101.8 all-gather.13
  122.9 36.4 all-gather.15
  161.5 49.2 all-gather.17
  212.8 123.4 all-gather.19
  338.3 123.1 all-gather.23
  463.4 123.1 all-gather.25
  588.7 47.4 all-gather.27
  829.5 94.8 all-reduce.13
  926.6 99.1 all-gather.29
  1029.3 86.1 reduce-scatter.15
  1119.4 207.0 reduce-scatter.13
  1330.6 281.7 reduce-scatter.17
  1616.2 281.7 reduce-scatter.19
  1900.2 123.9 all-gather.21
  2028.3 60.0 reduce-scatter.21
  2091.6 60.9 reduce-scatter.23
  2156.2 60.8 reduce-scatter.25
  2220.1 68.0 all-reduce.11
where the time goes:
time: 2310 us; the launch traced here: 2300 us
  waiting for transfers between devices  1660 us (72%)
  matrix products  269 us (12%)
  blocking collectives  181 us (8%)
  local copies, waits for them, and re-layouts  108 us (5%)
  other arithmetic  49 us (2%)
    reduce_scatter x1, waiting for transfers between devices, body(): lax.psum_scatter(grad_fc1, 'fsdp', scatter_dimension=0, tiled=True)  284 us
    reduce_scatter x1, waiting for transfers between devices, body(): lax.psum_scatter(grad_fc2, 'fsdp', scatter_dimension=0, tiled=True)  283 us
    unnamed x22, waiting for transfers between devices  227 us
    reduce_scatter x1, waiting for transfers between devices, body(): lax.psum_scatter(grad_qkv, 'fsdp', scatter_dimension=0, tiled=True)  209 us
    all_gather x1, waiting for transfers between devices, body(): lax.all_gather(fc2_weight, 'fsdp', axis=0, tiled=True)  123 us
    all_gather x1, waiting for transfers between devices, body(): lax.all_gather(held_fc2, 'fsdp', axis=0, tiled=True)  117 us
    all_gather x1, waiting for transfers between devices, body(): lax.all_gather(held_fc1, 'fsdp', axis=0, tiled=True)  115 us
    psum x1, waiting for transfers between devices, body(): lax.psum(qkv_part.astype(jnp.bfloat16), 'ctx').astype(jnp.float32)  61.3 us
  transfers between devices with their start and end apart: 18, of which 16 were waited for; matrix products, arithmetic and copies ran while one was open for 10% of the time, Pallas kernels for 0%

commit v1 on v0

--- a/solution.py
+++ b/solution.py
@@ -264,7 +264,7 @@
     finished = (
         lax.psum(gain_part.astype(jnp.bfloat16), "ctx").astype(jnp.float32),
         lax.psum(shift_part.astype(jnp.bfloat16), "ctx").astype(jnp.float32),
-        lax.psum(qkv_part.astype(jnp.bfloat16), "ctx").astype(jnp.float32),
+        jnp.sum(lax.all_gather(qkv_part.astype(jnp.bfloat16), "ctx"), axis=0).astype(jnp.float32),
         lax.psum(qv_part.astype(jnp.bfloat16), "ctx").astype(jnp.float32),
         lax.psum(out_part.astype(jnp.bfloat16), "ctx").astype(jnp.float32),
         lax.psum(out_shift_part.astype(jnp.bfloat16), "ctx").astype(jnp.float32),

time: 2310 us -> 2120 us (0.918)
  waiting for transfers between devices: 1660 us -> 1460 us
    reduce_scatter x1, waiting for transfers between devices: 284 us -> 181 us  [body(): lax.psum_scatter(grad_fc1, 'fsdp', scatter_dimension=0, tiled=True)]
    unnamed x22, waiting for transfers between devices: 227 us -> 304 us
    psum x1 -> x0, waiting for transfers between devices: 61.3 us -> none  [body(): lax.psum(qkv_part.astype(jnp.bfloat16), 'ctx').astype(jnp.float32)]
    reduce_scatter x1, waiting for transfers between devices: 59.5 us -> 0.01 us  [body(): lax.psum_scatter(grad_out_matrix, 'fsdp', scatter_dimension=0, tiled=True)]
    all_gather x1, waiting for transfers between devices: 123 us -> 69.6 us  [body(): lax.all_gather(fc2_weight, 'fsdp', axis=0, tiled=True)]
    all_gather x1, waiting for transfers between devices: 41.5 us -> 15 us  [body(): lax.all_gather(held_out, 'fsdp', axis=0, tiled=True)]
  transfers between devices with their start and end apart: 18 -> 18, of which waited for: 16 -> 15; matrix products, arithmetic and copies ran while one was open for 10% -> 19% of each run, Pallas kernels for 0% -> 0%
where the time goes in v1:
time: 2120 us; the launch traced here: 2110 us
  waiting for transfers between devices  1460 us (69%)
  matrix products  270 us (13%)
  blocking collectives  181 us (9%)
  local copies, waits for them, and re-layouts  107 us (5%)
  other arithmetic  48 us (2%)
  loops' own time  22.1 us (1%)
    unnamed x22, waiting for transfers between devices  304 us
    reduce_scatter x1, waiting for transfers between devices, body(): lax.psum_scatter(grad_fc2, 'fsdp', scatter_dimension=0, tiled=True)  283 us
    reduce_scatter x1, waiting for transfers between devices, body(): lax.psum_scatter(grad_qkv, 'fsdp', scatter_dimension=0, tiled=True)  201 us
    reduce_scatter x1, waiting for transfers between devices, body(): lax.psum_scatter(grad_fc1, 'fsdp', scatter_dimension=0, tiled=True)  181 us
    all_gather x1, waiting for transfers between devices, body(): lax.all_gather(held_fc2, 'fsdp', axis=0, tiled=True)  117 us
    all_gather x1, waiting for transfers between devices, body(): lax.all_gather(held_fc1, 'fsdp', axis=0, tiled=True)  115 us
    all_gather x1, waiting for transfers between devices, body(): lax.all_gather(held_qkv, 'fsdp', axis=0, tiled=True)  80 us
    all_gather x1, waiting for transfers between devices, body(): lax.all_gather(fc2_weight, 'fsdp', axis=0, tiled=True)  69.6 us
  transfers between devices with their start and end apart: 18, of which 15 were waited for; matrix products, arithmetic and copies ran while one was open for 19% of the time, Pallas kernels for 0%

profile of v1, /device:TPU:0, one launch (start us, length us, event | category | flops | bytes accessed | tf_op | source)
XLA Modules:
  0.0 2107.1 jit_solution(14461050748864809415)
XLA Ops:
  8.0 2.3 copy.94
  13.6 22.3 %all_gather.58 = bf16[2,1024]{1,0:T(2,128)(2,1)S(1)} all-gather(bf16[2,128]{1,0:T(2,128)(2,1)S(1)} %copy-done.13), channel_id=1, replica_groups=mesh['fsdp'=8,'ctx'=4] {'fsdp'}, dimensions={1}, use_global_device_ids=true | all-gather | bytes 4608 | tf_op jit(solution)/shard_map/all_gather | solution.py:58
  36.0 16.5 all_gather.59
  52.4 18.4 all_gather.61
  70.8 41.2 %all-gather.16.cloned.1.call-done = bf16[1024,3072]{1,0:T(8,128)(2,1)} async-done(((bf16[128,3072]{1,0:T(8,128)(2,1)}), bf16[1024,3072]{1,0:T(8,128)(2,1)}) %all-gather.16.cloned.1.call-update) | async-done | bytes 6291472 | tf_op jit(solution)/shard_map/all_gather | solution.py:60
  112.0 5.0 fusion.46
  120.5 2.3 copy.99
  127.8 5.1 all-gather.1
  133.0 17.6 all-gather.2
  150.6 26.1 %all-gather.3 = bf16[8,1,512]{2,1,0:T(2,128)(2,1)S(1)} all-gather(bf16[1,1,512]{2,1,0:T(2,128)(2,1)S(1)} %reshape.216), channel_id=1, replica_groups=mesh['fsdp'=8,'ctx'=4] {'fsdp'}, dimensions={0}, use_global_device_ids=true | all-gather | bytes 9216 | tf_op jit(solution)/shard_map/all_gather | solution.py:65
  176.7 16.7 all_gather.71
  194.2 11.7 copy.101
  205.8 88.4 %while.30 = (s32[]{:T(128)}, bf16[16,2,148,64]{2,3,1,0:T(8,128)(2,1)}, f32[16,2,148]{2,1,0:T(2,128)}, pred[2,1,592]{2,0,1:T(4,128)(4,1)S(1)}, s32[16]{0:T(128)S(...) while((s32[]{:T(128)}, ...), condition=%wide.region_5.6_spmd, body=%wide.region_2.5_spmd.sunk | while | flops 46279904 | bytes 2575710 | solution.py:119
  208.8 2.0 fusion.93
  219.9 2.0 fusion.93
  230.9 2.0 fusion.93
  236.4 2.0 fusion.93
  241.9 2.0 fusion.93
  247.5 2.0 fusion.93
  253.0 2.0 fusion.93
  264.1 2.0 fusion.93
  269.6 2.0 fusion.93
  294.3 2.2 copy.102
  298.2 2.7 fusion.54
  301.2 35.2 %all-gather.22.cloned.1.call-done = bf16[1024,4096]{1,0:T(8,128)(2,1)} async-done(((bf16[128,4096]{1,0:T(8,128)(2,1)}), bf16[1024,4096]{1,0:T(8,128)(2,1)}) %all-gather.22.cloned.1.call-update) | async-done | bytes 8388624 | tf_op jit(solution)/shard_map/all_gather | solution.py:64
  336.3 8.5 convolution_add_fusion
  344.8 116.7 %all-gather.26.cloned.1.call-done = bf16[4096,1024]{1,0:T(8,128)(2,1)} async-done(((bf16[512,1024]{1,0:T(8,128)(2,1)}), bf16[4096,1024]{1,0:T(8,128)(2,1)}) %all-gather.26.cloned.1.call-update) | async-done | bytes 8388624 | tf_op jit(solution)/shard_map/all_gather | solution.py:151
  461.5 10.3 fusion.55
  471.7 114.9 %all-gather.28.cloned.1.call-done = bf16[1024,4096]{1,0:T(8,128)(2,1)} async-done(((bf16[128,4096]{1,0:T(8,128)(2,1)}), bf16[1024,4096]{1,0:T(8,128)(2,1)}) %all-gather.28.cloned.1.call-update) | async-done | bytes 8388624 | tf_op jit(solution)/shard_map/all_gather | solution.py:150
  586.6 6.6 multiply_reduce_fusion.1
  594.7 3.4 fusion.42
  598.2 10.0 fusion.38
  608.3 13.0 fusion.47
  621.3 15.0 all-gather.30.cloned.1.call-done
  636.4 3.6 convolution_convert_fusion.1
  640.0 2.0 reshape.205
  642.0 2.2 copy.106
  644.2 165.5 %while.31 = (s32[]{:T(128)}, f32[16,2,148,64]{2,3,1,0:T(8,128)}, bf16[16,2,592,64]{2,3,1,0:T(8,128)(2,1)}, bf16[16,2,592,64]{2,3,1,0:T(8,128)(2,1)}, pred[2,1,59...) while((s32[]{:T(128)}, f32[16,2,148,64]{2,3,1,0:T(8,128)}, ...), condition=%wide.region_12.13_spmd, body=%wide.region_10.12_spmd.sunk | while | flops 113820000 | bytes 11655714 | solution.py:214
  809.7 3.7 copy.108
  813.3 6.6 copy.109
  819.9 3.5 copy.111
  823.4 6.7 copy.112
  831.9 181.3 %reduce-scatter.18.cloned.1.call-done = f32[128,4096]{1,0:T(8,128)} async-done(((f32[1024,4096]{1,0:T(8,128)}), f32[128,4096]{1,0:T(8,128)}) %reduce-scatter.18.cloned.1.call-update) | async-done | bytes 2097168 | tf_op jit(solution)/shard_map/reduce_scatter | solution.py:259
  1013.2 2.7 convert_element_type.219
  1015.9 282.8 %reduce-scatter.20.cloned.1.call-done = f32[512,1024]{1,0:T(8,128)} async-done(((f32[4096,1024]{1,0:T(8,128)}), f32[512,1024]{1,0:T(8,128)}) %reduce-scatter.20.cloned.1.call-update) | async-done | bytes 2097168 | tf_op jit(solution)/shard_map/reduce_scatter | solution.py:261
  1298.7 2.7 convert_element_type.223
  1305.3 2.0 copy.107
  1307.3 2.2 reshape.206
  1310.3 126.2 %all-reduce.10.cloned.1.call-done = (bf16[2,592,1024]{2,0,1:T(2,128)(2,1)}, bf16[2,592,1024]{2,0,1:T(2,128)(2,1)}, bf16[128,1024]{1,0:T(8,128)(2,1)}, bf16[128,4096]{1,0:T(8,128)(2,1)}, bf16[512,1024]{1,0:T(8,128)(2,1)}) async-done(((bf16[2,592,1024]{2,0,1:T(2,128)(2,1)}, bf16[2,592,1024]{2,0,1:T(2,128)(2,1)}, bf16[128,1024]{1,0:T(8,128)(2,1)}, bf16[128,4096]{1,0:T(8,128)(2,1)}, ...) | async-done | bytes 7208976
  1446.0 8.4 fusion.45
  1458.0 80.0 %all-gather.32.cloned.1.call-done = bf16[1024,3072]{1,0:T(8,128)(2,1)} async-done(((bf16[128,3072]{1,0:T(8,128)(2,1)}), bf16[1024,3072]{1,0:T(8,128)(2,1)}) %all-gather.32.cloned.1.call-update) | async-done | bytes 6291472 | tf_op jit(solution)/shard_map/all_gather | solution.py:148
  1538.0 6.7 multiply_reduce_fusion.2
  1547.0 200.7 %reduce-scatter.14.cloned.1.call-done = f32[128,3072]{1,0:T(8,128)} async-done(((f32[1024,3072]{1,0:T(8,128)}), f32[128,3072]{1,0:T(8,128)}) %reduce-scatter.14.cloned.1.call-update) | async-done | bytes 1572880 | tf_op jit(solution)/shard_map/reduce_scatter | solution.py:255
  1747.6 2.4 convert_element_type.210
  1752.0 18.5 all-gather.4
  1770.5 34.3 %all-reduce.5 = (bf16[1024]{0:T(1024)(128)(2,1)S(1)}, bf16[4096]{0:T(1024)(128)(2,1)S(1)}, bf16[1024]{0:T(1024)(128)(2,1)S(1)}) all-reduce(f32[1024]{0:T(1024)S(1)} %get-tuple-element.447, f32[4096]{0:T(1024)S(1)} %get-tuple-element.469, f32[1024]{0:T(1024)S(1)} %get-tuple-element.445), channel_id=10, replica_groups=mesh['fsdp'=8,'ctx'=4] {'fsdp'}, use_global_device_ids=true, to_apply=%region_34.35.clone | all-reduce | flops 6144 | bytes 36864
  1805.0 69.6 %all-gather.24.cloned.1.call-done = bf16[4096,1024]{1,0:T(8,128)(2,1)} async-done(((bf16[512,1024]{1,0:T(8,128)(2,1)}), bf16[4096,1024]{1,0:T(8,128)(2,1)}) %all-gather.24.cloned.1.call-update) | async-done | bytes 8388624 | tf_op jit(solution)/shard_map/all_gather | solution.py:66
  1874.6 8.5 fusion.35
  1891.9 46.4 %reduce-scatter.26.cloned.1.call-done = f32[128,2]{1,0:T(8,128)} async-done(((f32[1024,2]{1,0:T(8,128)}), f32[128,2]{1,0:T(8,128)}) %reduce-scatter.26.cloned.1.call-update) | async-done | bytes 1040
  1939.3 63.3 %reduce-scatter.24.cloned.1.call-done = f32[128,2]{1,0:T(8,128)} async-done(((f32[1024,2]{1,0:T(8,128)}), f32[128,2]{1,0:T(8,128)}) %reduce-scatter.24.cloned.1.call-update) | async-done | bytes 1040
  2003.5 63.6 %reduce-scatter.22.cloned.1.call-done = f32[128,2]{1,0:T(8,128)} async-done(((f32[1024,2]{1,0:T(8,128)}), f32[128,2]{1,0:T(8,128)}) %reduce-scatter.22.cloned.1.call-update) | async-done | bytes 1040
  2068.1 5.7 all-reduce.6
  2077.0 19.1 all-gather.34.cloned.1.call-done
  2096.2 2.5 reduce_sum.201
  (435 shorter events, 268.6 us)
Async XLA Ops:
  7.2 104.9 %all-gather.16.cloned.1.call-start = ((), (), s32[]{:S(2)}) async-start(), calls=%async_computation.7 | async-start | bytes 7077888 | tf_op jit(solution)/shard_map/all_gather | solution.py:60
  7.9 3.9 copy-start.2
  7.9 186.2 %all-gather.18.cloned.1.call-start = ((), (), s32[]{:S(2)}) async-start(), calls=%async_computation.8 | async-start | bytes 6062080 | tf_op jit(solution)/shard_map/all_gather | solution.py:96
  10.3 3.3 copy-start.13
  10.3 25.7 %copy-start.16 = (bf16[2,128]{1,0:T(2,128)(2,1)S(1)}, bf16[2,128]{1,0:T(2,128)(2,1)}, u32[]{:S(2)}) copy-start(bf16[2,128]{1,0:T(2,128)(2,1)} %param.23) | copy-start | bytes 1540
  10.3 42.1 %copy-start.17 = (bf16[2,128]{1,0:T(2,128)(2,1)S(1)}, bf16[2,128]{1,0:T(2,128)(2,1)}, u32[]{:S(2)}) copy-start(bf16[2,128]{1,0:T(2,128)(2,1)} %param.25) | copy-start | bytes 1540
  122.8 1.4 copy-start.20
  122.8 1.5 copy-start.11
  122.8 175.3 %all-gather.20.cloned.1.call-start = ((), (), s32[]{:S(2)}) async-start(), calls=%async_computation.9 | async-start | bytes 2359296 | tf_op jit(solution)/shard_map/all_gather | solution.py:62
  123.6 212.8 %all-gather.22.cloned.1.call-start = ((), (), s32[]{:S(2)}) async-start(), calls=%async_computation.10 | async-start | bytes 9437184 | tf_op jit(solution)/shard_map/all_gather | solution.py:64
  124.1 337.3 %all-gather.26.cloned.1.call-start = ((), (), s32[]{:S(2)}) async-start(), calls=%async_computation.12 | async-start | bytes 9437184 | tf_op jit(solution)/shard_map/all_gather | solution.py:151
  125.4 2.4 copy-start.14
  125.4 7.6 copy-start.18
  125.4 25.2 %copy-start.15 = (bf16[512]{0:T(512)(128)(2,1)S(1)}, bf16[512]{0:T(512)(128)(2,1)}, u32[]{:S(2)}) copy-start(bf16[512]{0:T(512)(128)(2,1)} %param.29) | copy-start | bytes 3076
  125.4 68.1 %copy-start.6 = (bf16[296,1024]{1,0:T(8,128)(2,1)S(1)}, bf16[296,1024]{1,0:T(8,128)(2,1)}, u32[]{:S(2)}) copy-start(bf16[296,1024]{1,0:T(8,128)(2,1)} %get-tuple-element.456) | copy-start | bytes 1818628
  126.4 460.2 %all-gather.28.cloned.1.call-start = ((), (), s32[]{:S(2)}) async-start(), calls=%async_computation.13 | async-start | bytes 9437184 | tf_op jit(solution)/shard_map/all_gather | solution.py:150
  127.0 509.4 %all-gather.30.cloned.1.call-start = ((), (), s32[]{:S(2)}) async-start(), calls=%async_computation.14 | async-start | bytes 2359296 | tf_op jit(solution)/shard_map/all_gather | solution.py:149
  127.7 702.4 %reduce-scatter.16.cloned.1.call-start = ((), (), s32[]{:S(2)}) async-start(), calls=%async_computation.17 | async-start | bytes 4718592 | tf_op jit(solution)/shard_map/reduce_scatter | solution.py:257
  586.6 6.6 copy-start.7
  593.2 1.5 copy-start.5
  598.1 415.1 %reduce-scatter.18.cloned.1.call-start = ((), (), s32[]{:S(2)}) async-start(), calls=%async_computation.18 | async-start | bytes 18874368 | tf_op jit(solution)/shard_map/reduce_scatter | solution.py:259
  608.2 690.5 %reduce-scatter.20.cloned.1.call-start = ((), (), s32[]{:S(2)}) async-start(), calls=%async_computation.19 | async-start | bytes 18874368 | tf_op jit(solution)/shard_map/reduce_scatter | solution.py:261
  621.3 815.2 %all-reduce.10.cloned.1.call-start = ((), (), s32[]{:S(2)}) async-start(), calls=%async_computation.24 | async-start | bytes 14417920
  644.2 1.3 copy-start.3
  649.2 5.4 copy-start.4
  654.5 1.3 copy-start.3
  659.5 5.4 copy-start.4
  669.9 5.4 copy-start.4
  675.2 1.3 copy-start.3
  680.2 5.4 copy-start.4
  685.6 1.3 copy-start.3
  690.5 5.4 copy-start.4
  695.9 1.3 copy-start.3
  700.9 5.4 copy-start.4
  711.2 5.4 copy-start.4
  716.6 1.3 copy-start.3
  721.5 5.4 copy-start.4
  731.9 5.4 copy-start.4
  737.3 1.3 copy-start.3
  742.2 5.4 copy-start.4
  747.6 1.3 copy-start.3
  752.5 5.4 copy-start.4
  757.9 1.3 copy-start.3
  762.9 5.4 copy-start.4
  773.2 5.4 copy-start.4
  778.6 1.3 copy-start.3
  783.6 5.4 copy-start.4
  789.0 1.3 copy-start.3
  793.9 5.4 copy-start.4
  804.2 5.4 copy-start.4
  1301.5 236.6 %all-gather.32.cloned.1.call-start = ((), (), s32[]{:S(2)}) async-start(), calls=%async_computation.15 | async-start | bytes 7077888 | tf_op jit(solution)/shard_map/all_gather | solution.py:148
  1302.0 445.6 %reduce-scatter.14.cloned.1.call-start = ((), (), s32[]{:S(2)}) async-start(), calls=%async_computation.16 | async-start | bytes 14155776 | tf_op jit(solution)/shard_map/reduce_scatter | solution.py:255
  1454.3 420.3 %all-gather.24.cloned.1.call-start = ((), (), s32[]{:S(2)}) async-start(), calls=%async_computation.11 | async-start | bytes 9437184 | tf_op jit(solution)/shard_map/all_gather | solution.py:66
  1454.9 483.5 %reduce-scatter.26.cloned.1.call-start = ((), (), s32[]{:S(2)}) async-start(), calls=%async_computation.23 | async-start | bytes 589824
  1458.0 544.6 %reduce-scatter.24.cloned.1.call-start = ((), (), s32[]{:S(2)}) async-start(), calls=%async_computation.22 | async-start | bytes 589824
  1545.8 521.4 %reduce-scatter.22.cloned.1.call-start = ((), (), s32[]{:S(2)}) async-start(), calls=%async_computation.21 | async-start | bytes 589824
  1546.9 203.2 %copy-start.21 = (u32[32]{0:T(128)S(1)}, u32[32]{0:T(128)}, u32[]{:S(2)}) copy-start(u32[32]{0:T(128)} %constant.164) | copy-start | bytes 388
  1546.9 205.1 %copy-start.19 = (bf16[128]{0:T(256)(128)(2,1)S(1)}, bf16[128]{0:T(256)(128)(2,1)}, u32[]{:S(2)}) copy-start(bf16[128]{0:T(256)(128)(2,1)} %param.31) | copy-start | bytes 772
  1546.9 549.3 %all-gather.34.cloned.1.call-start = ((), (), s32[]{:S(2)}) async-start(), calls=%async_computation.20 | async-start | bytes 3932160 | tf_op jit(solution)/shard_map/all_gather | solution.py:267
  1883.1 2.8 copy-start.1
  1884.4 1.5 copy-start.8
  1886.4 1.6 copy-start.10
  1888.0 1.5 copy-start.9
  1889.5 1.6 copy-start.12
  (7 other events, 8.6 us)
Sparse Core Ops, SparseCore 0:
  10.2 101.8 all-gather.15
  122.9 36.3 all-gather.17
  161.5 49.2 all-gather.19
  212.8 123.4 all-gather.21
  338.3 123.1 all-gather.25
  463.4 123.1 all-gather.27
  588.7 47.6 all-gather.29
  640.0 86.3 reduce-scatter.15
  730.7 282.4 reduce-scatter.17
  1016.8 281.8 reduce-scatter.19
  1302.2 134.2 all-reduce.9
  1438.8 99.2 all-gather.31
  1542.0 205.5 reduce-scatter.13
  1749.8 124.7 all-gather.23
  1878.2 60.1 reduce-scatter.25
  1941.6 60.9 reduce-scatter.23
  2006.1 60.9 reduce-scatter.21
  2068.6 27.5 all-gather.33
